TPU v7x, 256 devices: a whole 4x4x8 slice. The times are simulated.
256 devices in a mesh: seq: 128 (over x_lo, y, z, core), head: 2 (over x_hi).
Axes of the slice: x: 4 (x_hi: 2, x_lo: 2; x = x_hi * 2 + x_lo), y: 4, z: 8, core: 2. Of those that a mesh axis runs over, the one named last changes fastest.
Arguments:
- queries: bfloat16 [16384, 3072], P('seq', 'head'), may hold values from -6 to 6
- keys: bfloat16 [16384, 3072], P('seq', 'head'), may hold values from -6 to 6
- values: bfloat16 [16384, 3072], P('seq', 'head'), may hold values from -6 to 6
- cache_k: bfloat16 [2048, 3072], P('seq', 'head'), may hold values from -6 to 6
- cache_v: bfloat16 [2048, 3072], P('seq', 'head'), may hold values from -6 to 6
- sink_k: bfloat16 [8, 3072], P(None, 'head'), may hold values from -6 to 6
- sink_v: bfloat16 [8, 3072], P(None, 'head'), may hold values from -6 to 6
- suffix_lengths: int32 [32], replicated, may hold values from 1 to 1024, 16384 in all
- request_group: int32 [32], replicated, may hold values from 0 to 1
- w_out: bfloat16 [3072, 3072], P('head'), may hold values from -0.109375 to 0.109375
Outputs:
- projected: bfloat16 [3072, 16384], P('head', 'seq')
All inputs are finite; a program needn't handle non-finite values.
Results may differ from a plain program's by a relative error of at most 0.011.
Values may be sent and summed in bfloat16 or wider, within the bound.
No kernel may reach another device: no remote copies, remote signals or barrier semaphores. Data moves between devices by JAX's collectives and lax.ppermute only.
A program may use at most 128 MiB of HBM per device.

v0:
```python
import math
import jax
import jax.numpy as jnp
from jax import lax
from jax.sharding import PartitionSpec as P

HD = 96
W = 1024
SINKS = 4


def from_behind(array, axis, by):
    devices = lax.axis_size(axis)
    pairs = [(i, i + by) for i in range(devices) if 0 <= i + by < devices]
    return lax.ppermute(array, axis, pairs)


def describe(index, starts, lengths, groups):
    inside = (starts[None, :] <= index[:, None]) & (index[:, None] < (starts + lengths)[None, :])
    flag = inside.astype(jnp.int32)
    found = jnp.sum(flag, axis=1)
    request = jnp.sum(flag * jnp.arange(starts.shape[0], dtype=jnp.int32)[None, :], axis=1)
    request = jnp.where(found > 0, request, -1)
    offset = index - jnp.sum(flag * starts[None, :], axis=1)
    group = jnp.sum(flag * groups[None, :], axis=1)
    return (request, offset, group)


def shards(
    queries, keys, values, cache_k, cache_v, sink_k, sink_v, suffix_lengths, request_group, w_out
):
    rows, width = queries.shape
    heads = width // HD
    scale = 1.0 / math.sqrt(HD)
    device = lax.axis_index("seq")
    starts = jnp.cumsum(suffix_lengths) - suffix_lengths
    index = device * rows + jnp.arange(rows, dtype=jnp.int32)
    req_q, off_q, grp_q = describe(index, starts, suffix_lengths, request_group)
    q_three = queries.reshape(rows, heads, HD)

    def absorb(state, key_rows, value_rows, mask):
        top, den, acc = state
        count = key_rows.shape[0]
        k_three = key_rows.reshape(count, heads, HD)
        v_three = value_rows.reshape(count, heads, HD)
        score = (
            jnp.einsum("shd,khd->hsk", q_three, k_three, preferred_element_type=jnp.float32) * scale
        )
        score = jnp.where(mask[None], score, jnp.float32(-1e30))
        new_top = jnp.maximum(top, jnp.max(score, axis=2))
        factor = jnp.exp(top - new_top)
        prob = jnp.where(mask[None], jnp.exp(score - new_top[:, :, None]), jnp.float32(0.0))
        den = den * factor + jnp.sum(prob, axis=2)
        part = jnp.einsum(
            "hsk,khd->hsd", prob.astype(jnp.bfloat16), v_three, preferred_element_type=jnp.float32
        )
        acc = acc * factor[:, :, None] + part
        return (new_top, den, acc)

    def suffix_mask(near):
        req_k, off_k, grp_k = describe(near, starts, suffix_lengths, request_group)
        return (
            (req_k[None, :] == req_q[:, None])
            & (near[None, :] <= index[:, None])
            & (index[:, None] - near[None, :] < W)
            & (near[None, :] >= 0)
        )

    state = (
        jnp.full((heads, rows), -1e30, jnp.float32),
        jnp.zeros((heads, rows), jnp.float32),
        jnp.zeros((heads, rows, HD), jnp.float32),
    )
    sink_group = jnp.arange(sink_k.shape[0], dtype=jnp.int32) // SINKS
    state = absorb(state, sink_k, sink_v, grp_q[:, None] == sink_group[None, :])
    pieces = (
        lax.all_gather(cache_k, "seq", axis=0, tiled=True),
        lax.all_gather(cache_v, "seq", axis=0, tiled=True),
    )
    slot = jnp.arange(pieces[0].shape[0], dtype=jnp.int32)
    state = absorb(
        state,
        pieces[0],
        pieces[1],
        (grp_q[:, None] == (slot // W)[None, :]) & ((slot % W)[None, :] > off_q[:, None]),
    )
    state = absorb(state, keys, values, suffix_mask(index))
    reach = W // rows
    current = (keys, values)
    for step in range(1, reach + 1):
        current = from_behind((current[0], current[1]), "seq", 1)
        near = (device - step) * rows + jnp.arange(rows, dtype=jnp.int32)
        state = absorb(state, current[0], current[1], suffix_mask(near))
    top, den, acc = state
    attn = (acc / den[:, :, None]).transpose(1, 0, 2).reshape(rows, width).astype(jnp.bfloat16)
    return lax.psum_scatter(
        jnp.einsum("cd,sc->ds", w_out, attn, preferred_element_type=jnp.float32).astype(
            jnp.bfloat16
        ),
        "head",
        scatter_dimension=0,
        tiled=True,
    )


def solution(mesh):
    placed = (
        P("seq", "head"),
        P("seq", "head"),
        P("seq", "head"),
        P("seq", "head"),
        P("seq", "head"),
        P(None, "head"),
        P(None, "head"),
        P(),
        P(),
        P("head", None),
    )
    return jax.shard_map(
        shards, mesh=mesh, in_specs=placed, out_specs=P("head", "seq"), check_vma=False
    )
```

profile of v0, /device:TPU:1, one launch (start us, length us, event | category | flops | bytes accessed | tf_op | source)
XLA Modules:
  0.0 552.5 jit_solution(7046040993679264815)
XLA Ops:
  8.1 4.9 collective-permute-start
  13.0 1.9 collective-permute-start.1
  18.7 3.9 collective-permute-start.2
  22.7 3.8 collective-permute-start.3
  30.0 2.6 collective-permute-start.4
  33.2 4.4 collective-permute-start.5
  38.8 1.9 copy.96
  43.1 1.9 collective-permute-start.6
  45.1 3.9 collective-permute-start.7
  50.9 4.4 collective-permute-start.8
  55.3 4.3 collective-permute-start.9
  62.6 1.9 copy.101
  64.5 2.3 collective-permute-start.10
  66.9 4.4 collective-permute-start.11
  71.3 2.0 fusion.168
  75.2 1.9 copy.104
  77.1 1.9 copy.105
  79.0 3.0 fusion.167
  82.0 1.9 copy.107
  83.9 2.9 collective-permute-start.12
  86.8 4.4 collective-permute-start.13
  91.2 2.9 fusion.166
  94.1 1.9 copy.108
  96.0 1.9 copy.110
  97.9 1.9 copy.111
  99.9 2.9 fusion.165
  102.8 1.9 copy.113
  104.7 3.3 collective-permute-start.14
  108.0 4.7 collective-permute-start.15
  112.7 3.0 fusion.164
  115.7 1.9 copy.114
  117.6 1.9 copy.116
  119.5 1.9 copy.117
  121.5 2.9 fusion.163
  124.4 1.9 copy.119
  126.3 1.9 copy.120
  128.2 3.0 fusion.162
  131.2 144.8 %all-gather.3.cloned.1.call-done = bf16[2048,1536]{1,0:T(8,128)(2,1)} async-done(((bf16[16,1536]{1,0:T(8,128)(2,1)}), bf16[2048,1536]{1,0:T(8,128)(2,1)}) %all-gather.3.cloned.1.call-update) | async-done | bytes 6291472 | tf_op jit(solution)/shard_map/all_gather | solution.py:77
  276.0 8.7 %copy.93 = bf16[2048,1536]{0,1:T(8,128)(2,1)} copy(bf16[2048,1536]{1,0:T(8,128)(2,1)} %all-gather.3.cloned.1.call-done) | data formatting | bytes 12582912 | tf_op jit(solution)/shard_map/all_gather | solution.py:77
  284.8 5.8 %fusion = (f32[16,128]{1,0:T(8,128)S(1)}, f32[16,128,2048]{2,1,0:T(8,128)S(1)}) fusion(pred[128,2048]{1,0:T(8,128)(4,1)} %compare_and_fusion, bf16[128,16,96]{0,2,1:T(8,128)(2,1)S(1)} %bitcast.301, bf16[2048,16,96]{0,2,1:T(8,128)(2,1)} %bitcast.302), kind=kOutput, calls=%fused_computation.2 | convolution fusion | flops 817887232 | bytes 23732224 | tf_op jit(solution)/shard_map/shd,khd->hsk/dot_general | solution.py:47
  291.9 4.4 copy-done
  296.3 5.6 %fusion.1 = f32[16,128]{1,0:T(8,128)} fusion(f32[16,128,2048]{2,1,0:T(8,128)S(1)} %get-tuple-element.97, f32[16,128]{1,0:T(8,128)S(1)} %get-tuple-element.62, pred[128,2048]{1,0:T(8,128)(4,1)S(1)} %copy-done.6), kind=kLoop, calls=%fused_computation.3 | loop fusion | flops 20969472 | bytes 17055744 | tf_op jit(solution)/shard_map/reduce_sum | solution.py:53
  301.9 188.9 %all-gather.5.cloned.1.call-done = bf16[2048,1536]{1,0:T(8,128)(2,1)} async-done(((bf16[16,1536]{1,0:T(8,128)(2,1)}), bf16[2048,1536]{1,0:T(8,128)(2,1)}) %all-gather.5.cloned.1.call-update) | async-done | bytes 6291472 | tf_op jit(solution)/shard_map/all_gather | solution.py:78
  490.9 8.7 %copy.94 = bf16[2048,1536]{0,1:T(8,128)(2,1)} copy(bf16[2048,1536]{1,0:T(8,128)(2,1)} %all-gather.5.cloned.1.call-done) | data formatting | bytes 12582912 | tf_op jit(solution)/shard_map/all_gather | solution.py:78
  499.8 10.3 %fusion.38 = f32[128,16,96]{0,2,1:T(8,128)S(1)} fusion(bf16[2048,16,96]{0,2,1:T(8,128)(2,1)} %bitcast.305, f32[16,128,2048]{2,1,0:T(8,128)} %copy-done, f32[16,128]{1,0:T(8,128)} %copy-done.55, pred[128,2048]{1,0:T(8,128)(4,1)S(1)} %copy-done.7), kind=kOutput, calls=%fused_computation.59 | convolution fusion | flops 826277888 | bytes 24125440 | tf_op jit(solution)/shard_map/hsk,khd->hsd/dot_general | solution.py:54
  518.6 2.3 fusion.6
  520.9 23.1 %reduce-scatter.2.cloned.1.call-done = bf16[1536,128]{0,1:T(8,128)(2,1)} async-done(((bf16[3072,128]{0,1:T(8,128)(2,1)}), bf16[1536,128]{0,1:T(8,128)(2,1)}) %reduce-scatter.2.cloned.1.call-update) | async-done | bytes 393232 | tf_op jit(solution)/shard_map/reduce_scatter | solution.py:96
  544.0 1.9 copy.122
  (208 shorter events, 29.0 us)
Async XLA Ops:
  6.5 269.5 %all-gather.3.cloned.1.call-start = ((), (), s32[]{:S(2)}) async-start(), calls=%async_computation.1 | async-start | bytes 6340608 | tf_op jit(solution)/shard_map/all_gather | solution.py:77
  7.3 483.6 %all-gather.5.cloned.1.call-start = ((), (), s32[]{:S(2)}) async-start(), calls=%async_computation.2 | async-start | bytes 6340608 | tf_op jit(solution)/shard_map/all_gather | solution.py:78
  8.0 536.0 %reduce-scatter.2.cloned.1.call-start = ((), (), s32[]{:S(2)}) async-start(), calls=%async_computation.3 | async-start | bytes 1179648 | tf_op jit(solution)/shard_map/reduce_scatter | solution.py:96
  8.1 10.7 %collective-permute-start = (bf16[128,1536]{1,0:T(8,128)(2,1)}, bf16[128,1536]{1,0:T(8,128)(2,1)S(1)}, u32[]{:S(2)}, u32[]{:S(2)}) collective-permute-start(bf16[128,1536]{1,0:T(8,128)(2,1)} %param.11), channel_id=1, source_target_pairs={{0,2},{2,4},{4,6},{6,8},{8,10},{10,12},{12,14},{14,16},{16,18},{18... | collective-permute-start | bytes 1179656 | tf_op jit(solution)/shard_map/ppermute | solution.py:15
  13.0 9.7 %collective-permute-start.1 = (bf16[128,1536]{1,0:T(8,128)(2,1)}, bf16[128,1536]{1,0:T(8,128)(2,1)S(1)}, u32[]{:S(2)}, u32[]{:S(2)}) collective-permute-start(bf16[128,1536]{1,0:T(8,128)(2,1)} %param.12), channel_id=1, source_target_pairs={{0,2},{2,4},{4,6},{6,8},{8,10},{10,12},{12,14},{14,16},{16,18},{18... | collective-permute-start | bytes 1179656 | tf_op jit(solution)/shard_map/ppermute | solution.py:15
  17.5 42.1 %copy-start.57 = (pred[128,8]{0,1:T(8,128)(4,1)}, pred[128,8]{0,1:T(8,128)(4,1)S(1)}, u32[]{:S(2)}) copy-start(pred[128,8]{0,1:T(8,128)(4,1)S(1)} %broadcast_compare_fusion) | copy-start | bytes 3076
  18.7 40.9 %copy-start.27 = (pred[128,128]{0,1:T(8,128)(4,1)}, pred[128,128]{0,1:T(8,128)(4,1)S(1)}, u32[]{:S(2)}) copy-start(pred[128,128]{0,1:T(8,128)(4,1)S(1)} %get-tuple-element.69) | copy-start | bytes 49156
  18.7 11.3 %collective-permute-start.2 = (bf16[128,1536]{1,0:T(8,128)(2,1)S(1)}, bf16[128,1536]{1,0:T(8,128)(2,1)}, u32[]{:S(2)}, u32[]{:S(2)}) collective-permute-start(bf16[128,1536]{1,0:T(8,128)(2,1)S(1)} %collective-permute-done), channel_id=1, source_target_pairs={{0,2},{2,4},{4,6},{6,8},{8,10},{10,12},{12,14},{14,16},{16,18},{18... | collective-permute-start | bytes 1179656 | tf_op jit(solution)/shard_map/ppermute | solution.py:15
  22.7 10.5 %collective-permute-start.3 = (bf16[128,1536]{1,0:T(8,128)(2,1)S(1)}, bf16[128,1536]{1,0:T(8,128)(2,1)S(1)}, u32[]{:S(2)}, u32[]{:S(2)}) collective-permute-start(bf16[128,1536]{1,0:T(8,128)(2,1)S(1)} %collective-permute-done.1), channel_id=1, source_target_pairs={{0,2},{2,4},{4,6},{6,8},{8,10},{10,12},{12,14},{14,16},{16,18},{18... | collective-permute-start | bytes 1179656 | tf_op jit(solution)/shard_map/ppermute | solution.py:15
  30.0 13.1 %collective-permute-start.4 = (bf16[128,1536]{1,0:T(8,128)(2,1)}, bf16[128,1536]{1,0:T(8,128)(2,1)}, u32[]{:S(2)}, u32[]{:S(2)}) collective-permute-start(bf16[128,1536]{1,0:T(8,128)(2,1)} %collective-permute-done.2), channel_id=1, source_target_pairs={{0,2},{2,4},{4,6},{6,8},{8,10},{10,12},{12,14},{14,16},{16,18},{18... | collective-permute-start | bytes 1179656 | tf_op jit(solution)/shard_map/ppermute | solution.py:15
  33.2 26.5 %copy-start.19 = (bf16[128,1536]{1,0:T(8,128)(2,1)}, bf16[128,1536]{1,0:T(8,128)(2,1)S(1)}, u32[]{:S(2)}) copy-start(bf16[128,1536]{1,0:T(8,128)(2,1)S(1)} %collective-permute-done.3) | copy-start | bytes 1179652
  33.2 11.9 %collective-permute-start.5 = (bf16[128,1536]{1,0:T(8,128)(2,1)S(1)}, bf16[128,1536]{1,0:T(8,128)(2,1)}, u32[]{:S(2)}, u32[]{:S(2)}) collective-permute-start(bf16[128,1536]{1,0:T(8,128)(2,1)S(1)} %collective-permute-done.3), channel_id=1, source_target_pairs={{0,2},{2,4},{4,6},{6,8},{8,10},{10,12},{12,14},{14,16},{16,18},{18... | collective-permute-start | bytes 1179656 | tf_op jit(solution)/shard_map/ppermute | solution.py:15
  43.1 7.8 %collective-permute-start.6 = (bf16[128,1536]{1,0:T(8,128)(2,1)}, bf16[128,1536]{1,0:T(8,128)(2,1)}, u32[]{:S(2)}, u32[]{:S(2)}) collective-permute-start(bf16[128,1536]{1,0:T(8,128)(2,1)} %collective-permute-done.4), channel_id=1, source_target_pairs={{0,2},{2,4},{4,6},{6,8},{8,10},{10,12},{12,14},{14,16},{16,18},{18... | collective-permute-start | bytes 1179656 | tf_op jit(solution)/shard_map/ppermute | solution.py:15
  45.1 10.2 %collective-permute-start.7 = (bf16[128,1536]{1,0:T(8,128)(2,1)}, bf16[128,1536]{1,0:T(8,128)(2,1)}, u32[]{:S(2)}, u32[]{:S(2)}) collective-permute-start(bf16[128,1536]{1,0:T(8,128)(2,1)} %collective-permute-done.5), channel_id=1, source_target_pairs={{0,2},{2,4},{4,6},{6,8},{8,10},{10,12},{12,14},{14,16},{16,18},{18... | collective-permute-start | bytes 1179656 | tf_op jit(solution)/shard_map/ppermute | solution.py:15
  50.9 13.6 %collective-permute-start.8 = (bf16[128,1536]{1,0:T(8,128)(2,1)}, bf16[128,1536]{1,0:T(8,128)(2,1)}, u32[]{:S(2)}, u32[]{:S(2)}) collective-permute-start(bf16[128,1536]{1,0:T(8,128)(2,1)} %collective-permute-done.6), channel_id=1, source_target_pairs={{0,2},{2,4},{4,6},{6,8},{8,10},{10,12},{12,14},{14,16},{16,18},{18... | collective-permute-start | bytes 1179656 | tf_op jit(solution)/shard_map/ppermute | solution.py:15
  55.3 11.6 %collective-permute-start.9 = (bf16[128,1536]{1,0:T(8,128)(2,1)}, bf16[128,1536]{1,0:T(8,128)(2,1)}, u32[]{:S(2)}, u32[]{:S(2)}) collective-permute-start(bf16[128,1536]{1,0:T(8,128)(2,1)} %collective-permute-done.7), channel_id=1, source_target_pairs={{0,2},{2,4},{4,6},{6,8},{8,10},{10,12},{12,14},{14,16},{16,18},{18... | collective-permute-start | bytes 1179656 | tf_op jit(solution)/shard_map/ppermute | solution.py:15
  64.5 19.4 %collective-permute-start.10 = (bf16[128,1536]{1,0:T(8,128)(2,1)}, bf16[128,1536]{1,0:T(8,128)(2,1)}, u32[]{:S(2)}, u32[]{:S(2)}) collective-permute-start(bf16[128,1536]{1,0:T(8,128)(2,1)} %collective-permute-done.8), channel_id=1, source_target_pairs={{0,2},{2,4},{4,6},{6,8},{8,10},{10,12},{12,14},{14,16},{16,18},{18... | collective-permute-start | bytes 1179656 | tf_op jit(solution)/shard_map/ppermute | solution.py:15
  66.9 19.9 %collective-permute-start.11 = (bf16[128,1536]{1,0:T(8,128)(2,1)}, bf16[128,1536]{1,0:T(8,128)(2,1)}, u32[]{:S(2)}, u32[]{:S(2)}) collective-permute-start(bf16[128,1536]{1,0:T(8,128)(2,1)} %collective-permute-done.9), channel_id=1, source_target_pairs={{0,2},{2,4},{4,6},{6,8},{8,10},{10,12},{12,14},{14,16},{16,18},{18... | collective-permute-start | bytes 1179656 | tf_op jit(solution)/shard_map/ppermute | solution.py:15
  83.9 20.8 %collective-permute-start.12 = (bf16[128,1536]{1,0:T(8,128)(2,1)}, bf16[128,1536]{1,0:T(8,128)(2,1)}, u32[]{:S(2)}, u32[]{:S(2)}) collective-permute-start(bf16[128,1536]{1,0:T(8,128)(2,1)} %collective-permute-done.10), channel_id=1, source_target_pairs={{0,2},{2,4},{4,6},{6,8},{8,10},{10,12},{12,14},{14,16},{16,18},{18... | collective-permute-start | bytes 1179656 | tf_op jit(solution)/shard_map/ppermute | solution.py:15
  86.8 21.2 %collective-permute-start.13 = (bf16[128,1536]{1,0:T(8,128)(2,1)}, bf16[128,1536]{1,0:T(8,128)(2,1)}, u32[]{:S(2)}, u32[]{:S(2)}) collective-permute-start(bf16[128,1536]{1,0:T(8,128)(2,1)} %collective-permute-done.11), channel_id=1, source_target_pairs={{0,2},{2,4},{4,6},{6,8},{8,10},{10,12},{12,14},{14,16},{16,18},{18... | collective-permute-start | bytes 1179656 | tf_op jit(solution)/shard_map/ppermute | solution.py:15
  104.7 19.7 %collective-permute-start.14 = (bf16[128,1536]{1,0:T(8,128)(2,1)}, bf16[128,1536]{1,0:T(8,128)(2,1)}, u32[]{:S(2)}, u32[]{:S(2)}) collective-permute-start(bf16[128,1536]{1,0:T(8,128)(2,1)} %collective-permute-done.12), channel_id=1, source_target_pairs={{0,2},{2,4},{4,6},{6,8},{8,10},{10,12},{12,14},{14,16},{16,18},{18... | collective-permute-start | bytes 1179656 | tf_op jit(solution)/shard_map/ppermute | solution.py:15
  108.0 18.3 %collective-permute-start.15 = (bf16[128,1536]{1,0:T(8,128)(2,1)}, bf16[128,1536]{1,0:T(8,128)(2,1)}, u32[]{:S(2)}, u32[]{:S(2)}) collective-permute-start(bf16[128,1536]{1,0:T(8,128)(2,1)} %collective-permute-done.13), channel_id=1, source_target_pairs={{0,2},{2,4},{4,6},{6,8},{8,10},{10,12},{12,14},{14,16},{16,18},{18... | collective-permute-start | bytes 1179656 | tf_op jit(solution)/shard_map/ppermute | solution.py:15
  284.8 11.6 %copy-start.6 = (pred[128,2048]{1,0:T(8,128)(4,1)S(1)}, pred[128,2048]{1,0:T(8,128)(4,1)}, u32[]{:S(2)}) copy-start(pred[128,2048]{1,0:T(8,128)(4,1)} %compare_and_fusion) | copy-start | bytes 786436
  290.6 208.9 %copy-start.7 = (pred[128,2048]{1,0:T(8,128)(4,1)S(1)}, pred[128,2048]{1,0:T(8,128)(4,1)}, u32[]{:S(2)}) copy-start(pred[128,2048]{1,0:T(8,128)(4,1)} %compare_and_fusion) | copy-start | bytes 786436
  291.9 207.6 %copy-start.55 = (f32[16,128]{1,0:T(8,128)}, f32[16,128]{1,0:T(8,128)S(1)}, u32[]{:S(2)}) copy-start(f32[16,128]{1,0:T(8,128)S(1)} %get-tuple-element.62) | copy-start | bytes 24580
  499.6 11.3 %copy-start.3 = (f32[16,128,128]{1,2,0:T(8,128)S(1)}, f32[16,128,128]{1,2,0:T(8,128)}, u32[]{:S(2)}) copy-start(f32[16,128,128]{1,2,0:T(8,128)} %get-tuple-element.85) | copy-start | bytes 3145732
  499.6 11.3 %copy-start.24 = (pred[128,128]{0,1:T(8,128)(4,1)S(1)}, pred[128,128]{0,1:T(8,128)(4,1)}, u32[]{:S(2)}) copy-start(pred[128,128]{0,1:T(8,128)(4,1)} %get-tuple-element.70) | copy-start | bytes 49156
  499.6 11.3 %copy-start.41 = (f32[16,128]{1,0:T(8,128)S(1)}, f32[16,128]{1,0:T(8,128)}, u32[]{:S(2)}) copy-start(f32[16,128]{1,0:T(8,128)} %get-tuple-element.56) | copy-start | bytes 24580
  499.6 11.5 %copy-start.2 = (f32[16,128,128]{1,2,0:T(8,128)S(1)}, f32[16,128,128]{1,2,0:T(8,128)}, u32[]{:S(2)}) copy-start(f32[16,128,128]{1,2,0:T(8,128)} %get-tuple-element.87) | copy-start | bytes 3145732
  499.7 11.5 %copy-start.42 = (f32[16,128]{1,0:T(8,128)S(1)}, f32[16,128]{1,0:T(8,128)}, u32[]{:S(2)}) copy-start(f32[16,128]{1,0:T(8,128)} %get-tuple-element.57) | copy-start | bytes 24580
  499.7 11.7 %copy-start.1 = (f32[16,128,128]{1,2,0:T(8,128)S(1)}, f32[16,128,128]{1,2,0:T(8,128)}, u32[]{:S(2)}) copy-start(f32[16,128,128]{1,2,0:T(8,128)} %get-tuple-element.89) | copy-start | bytes 3145732
  499.7 11.7 %copy-start.25 = (pred[128,128]{0,1:T(8,128)(4,1)S(1)}, pred[128,128]{0,1:T(8,128)(4,1)}, u32[]{:S(2)}) copy-start(pred[128,128]{0,1:T(8,128)(4,1)} %get-tuple-element.73) | copy-start | bytes 49156
  499.7 11.7 %copy-start.43 = (f32[16,128]{1,0:T(8,128)S(1)}, f32[16,128]{1,0:T(8,128)}, u32[]{:S(2)}) copy-start(f32[16,128]{1,0:T(8,128)} %get-tuple-element.58) | copy-start | bytes 24580
  499.7 11.9 %copy-start.26 = (pred[128,128]{0,1:T(8,128)(4,1)S(1)}, pred[128,128]{0,1:T(8,128)(4,1)}, u32[]{:S(2)}) copy-start(pred[128,128]{0,1:T(8,128)(4,1)} %get-tuple-element.71) | copy-start | bytes 49156
  499.7 11.9 %copy-start.44 = (f32[16,128]{1,0:T(8,128)S(1)}, f32[16,128]{1,0:T(8,128)}, u32[]{:S(2)}) copy-start(f32[16,128]{1,0:T(8,128)} %get-tuple-element.59) | copy-start | bytes 24580
  499.7 12.1 %copy-start.21 = (pred[128,128]{0,1:T(8,128)(4,1)S(1)}, pred[128,128]{0,1:T(8,128)(4,1)}, u32[]{:S(2)}) copy-start(pred[128,128]{0,1:T(8,128)(4,1)} %copy-done.20) | copy-start | bytes 49156
  499.7 12.1 %copy-start.45 = (f32[16,128]{1,0:T(8,128)S(1)}, f32[16,128]{1,0:T(8,128)}, u32[]{:S(2)}) copy-start(f32[16,128]{1,0:T(8,128)} %get-tuple-element.60) | copy-start | bytes 24580
  499.7 12.3 %copy-start.28 = (pred[128,128]{0,1:T(8,128)(4,1)S(1)}, pred[128,128]{0,1:T(8,128)(4,1)}, u32[]{:S(2)}) copy-start(pred[128,128]{0,1:T(8,128)(4,1)} %copy-done.27) | copy-start | bytes 49156
  499.7 12.3 %copy-start.46 = (f32[16,128]{1,0:T(8,128)S(1)}, f32[16,128]{1,0:T(8,128)}, u32[]{:S(2)}) copy-start(f32[16,128]{1,0:T(8,128)} %get-tuple-element.61) | copy-start | bytes 24580
  499.8 12.5 %copy-start.17 = (f32[16,128,8]{1,2,0:T(8,128)S(1)}, f32[16,128,8]{1,2,0:T(8,128)}, u32[]{:S(2)}) copy-start(f32[16,128,8]{1,2,0:T(8,128)} %get-tuple-element.99) | copy-start | bytes 196612
  499.8 13.5 %copy-start.31 = (f32[16,128]{1,0:T(8,128)S(1)}, f32[16,128]{1,0:T(8,128)}, u32[]{:S(2)}) copy-start(f32[16,128]{1,0:T(8,128)} %get-tuple-element.98) | copy-start | bytes 24580
  499.8 13.5 %copy-start.33 = (f32[16,128]{1,0:T(8,128)S(1)}, f32[16,128]{1,0:T(8,128)}, u32[]{:S(2)}) copy-start(f32[16,128]{1,0:T(8,128)} %get-tuple-element.92) | copy-start | bytes 24580
  499.8 13.5 %copy-start.35 = (f32[16,128]{1,0:T(8,128)S(1)}, f32[16,128]{1,0:T(8,128)}, u32[]{:S(2)}) copy-start(f32[16,128]{1,0:T(8,128)} %get-tuple-element.88) | copy-start | bytes 24580
  499.8 13.5 %copy-start.37 = (f32[16,128]{1,0:T(8,128)S(1)}, f32[16,128]{1,0:T(8,128)}, u32[]{:S(2)}) copy-start(f32[16,128]{1,0:T(8,128)} %copy-done.36) | copy-start | bytes 24580
  499.8 13.5 %copy-start.49 = (f32[16,128]{1,0:T(8,128)S(1)}, f32[16,128]{1,0:T(8,128)}, u32[]{:S(2)}) copy-start(f32[16,128]{1,0:T(8,128)} %get-tuple-element.84) | copy-start | bytes 24580
  499.8 14.3 %copy-start.38 = (bf16[8,16,96]{2,1,0:T(8,128)(2,1)S(1)}, bf16[8,16,96]{2,1,0:T(8,128)(2,1)}, u32[]{:S(2)}) copy-start(bf16[8,16,96]{2,1,0:T(8,128)(2,1)} %reshape.1640) | copy-start | bytes 73732
  499.8 15.4 %copy-start.9 = (bf16[128,1536]{0,1:T(8,128)(2,1)S(1)}, bf16[128,1536]{0,1:T(8,128)(2,1)}, u32[]{:S(2)}) copy-start(bf16[128,1536]{0,1:T(8,128)(2,1)} %copy.96) | copy-start | bytes 1179652
  499.8 15.7 %copy-start.10 = (bf16[128,1536]{0,1:T(8,128)(2,1)S(1)}, bf16[128,1536]{0,1:T(8,128)(2,1)}, u32[]{:S(2)}) copy-start(bf16[128,1536]{0,1:T(8,128)(2,1)} %copy.99) | copy-start | bytes 1179652
  (32 other events, 234.2 us)
Sparse Core Ops, SparseCore 0:
  9.2 266.7 all-gather.2
  277.9 212.9 all-gather.4
  521.1 22.9 reduce-scatter.1
where the time goes:
time: 554 us; the launch traced here: 552 us
  waiting for transfers between devices  360 us (65%)
  local copies, waits for them, and re-layouts  59.7 us (11%)
  starting transfers between devices  58.2 us (11%)
  matrix products  45.1 us (8%)
  other arithmetic  15.2 us (3%)
  between operations  14.5 us (3%)
    all_gather x1, waiting for transfers between devices, shards(): lax.all_gather(cache_v, 'seq', axis=0, tiled=True)  189 us
    all_gather x1, waiting for transfers between devices, shards(): lax.all_gather(cache_k, 'seq', axis=0, tiled=True)  145 us
    ppermute x16, starting transfers between devices, from_behind(): return lax.ppermute(array, axis, pairs)  58.1 us
    dot_general x11, matrix products, absorb(): jnp.einsum('shd,khd->hsk', q_three, k_three, preferred_element_type=jnp.f...  28.8 us
    ppermute x16, local copies, waits for them, and re-layouts, from_behind(): return lax.ppermute(array, axis, pairs)  28 us
    reduce_scatter x1, waiting for transfers between devices, shards(): lax.psum_scatter(jnp.einsum('cd,sc->ds', w_out, attn, preferred_element_t...  23.1 us
    dot_general x11, matrix products, absorb(): jnp.einsum('hsk,khd->hsd', prob.astype(jnp.bfloat16), v_three, preferred_...  14.1 us
  transfers between devices with their start and end apart: 19, of which 5 were waited for; matrix products, arithmetic and copies ran while one was open for 15% of the time, Pallas kernels for 0%

commit v1 on v0

--- a/solution.py
+++ b/solution.py
@@ -74,7 +74,9 @@
     sink_group = jnp.arange(sink_k.shape[0], dtype=jnp.int32) // SINKS
     state = absorb(state, sink_k, sink_v, grp_q[:, None] == sink_group[None, :])
     pieces = (
-        lax.all_gather(cache_k, "seq", axis=0, tiled=True),
+        jnp.concatenate(
+            lax.all_to_all(jnp.stack([cache_k] * lax.axis_size("seq")), "seq", 0, 0), axis=0
+        ),
         lax.all_gather(cache_v, "seq", axis=0, tiled=True),
     )
     slot = jnp.arange(pieces[0].shape[0], dtype=jnp.int32)

time: 554 us -> 381 us (0.69)
  waiting for transfers between devices: 360 us -> 176 us
  starting transfers between devices: 58.2 us -> 74.7 us
  local copies, waits for them, and re-layouts: 59.7 us -> 53.8 us
    all_gather x1, waiting for transfers between devices: 189 us -> 0.01 us  [shards(): lax.all_gather(cache_v, 'seq', axis=0, tiled=True)]
    ppermute x16, waiting for transfers between devices: 1.49 us -> 153 us  [from_behind(): return lax.ppermute(array, axis, pairs)]
    all_gather x1 -> x0, waiting for transfers between devices: 145 us -> none  [shards(): lax.all_gather(cache_k, 'seq', axis=0, tiled=True)]
    another operation x1 -> x3, local copies, waits for them, and re-layouts: 0.74 us -> 18.1 us  [the longest x1 13.6 us: absorb(): k_three = key_rows.reshape(count, heads, HD)]
    all_to_all x0 -> x1, starting transfers between devices: none -> 15.3 us  [shards(): lax.all_to_all(jnp.stack([cache_k] * lax.axis_size('seq')), 'seq', 0, 0)]
    all_gather x1 -> x0, local copies, waits for them, and re-layouts: 8.66 us -> none  [shards(): lax.all_gather(cache_k, 'seq', axis=0, tiled=True)]
    ppermute x16, local copies, waits for them, and re-layouts: 28 us -> 21.1 us  [from_behind(): return lax.ppermute(array, axis, pairs)]
    unnamed x125 -> x115, local copies, waits for them, and re-layouts: 9.45 us -> 3.23 us
  transfers between devices with their start and end apart: 19 -> 19, of which waited for: 5 -> 6; matrix products, arithmetic and copies ran while one was open for 15% -> 20% of each run, Pallas kernels for 0% -> 0%
where the time goes in v1:
time: 381 us; the launch traced here: 379 us
  waiting for transfers between devices  176 us (46%)
  starting transfers between devices  74.7 us (20%)
  local copies, waits for them, and re-layouts  53.8 us (14%)
  matrix products  42.2 us (11%)
  other arithmetic  17 us (4%)
  between operations  14.8 us (4%)
    ppermute x16, waiting for transfers between devices, from_behind(): return lax.ppermute(array, axis, pairs)  153 us
    ppermute x16, starting transfers between devices, from_behind(): return lax.ppermute(array, axis, pairs)  59.4 us
    dot_general x11, matrix products, absorb(): jnp.einsum('shd,khd->hsk', q_three, k_three, preferred_element_type=jnp.f...  25.9 us
    reduce_scatter x1, waiting for transfers between devices, shards(): lax.psum_scatter(jnp.einsum('cd,sc->ds', w_out, attn, preferred_element_t...  22.3 us
    ppermute x16, local copies, waits for them, and re-layouts, from_behind(): return lax.ppermute(array, axis, pairs)  21.1 us
    all_to_all x1, starting transfers between devices, shards(): lax.all_to_all(jnp.stack([cache_k] * lax.axis_size('seq')), 'seq', 0, 0)  15.3 us
    dot_general x11, matrix products, absorb(): jnp.einsum('hsk,khd->hsd', prob.astype(jnp.bfloat16), v_three, preferred_...  14 us
    another operation x1, local copies, waits for them, and re-layouts, absorb(): k_three = key_rows.reshape(count, heads, HD)  13.6 us
  transfers between devices with their start and end apart: 19, of which 6 were waited for; matrix products, arithmetic and copies ran while one was open for 20% of the time, Pallas kernels for 0%

profile of v1, /device:TPU:1, one launch (start us, length us, event | category | flops | bytes accessed | tf_op | source)
XLA Modules:
  0.0 378.7 jit_solution(4675555581239065956)
XLA Ops:
  6.6 4.3 %stack.2 = bf16[128,16,1536]{2,1,0:T(8,128)(2,1)} broadcast(bf16[16,1536]{1,0:T(8,128)(2,1)} %param.13), dimensions={1,2} | broadcast | bytes 6340608 | tf_op jit(solution)/shard_map/stack | solution.py:78
  10.9 15.3 %all-to-all-start = ((bf16[128,16,1536]{2,1,0:T(8,128)(2,1)}), bf16[128,16,1536]{2,1,0:T(8,128)(2,1)}, u32[]{:S(2)}, u32[]{:S(2)}) async-start(bf16[128,16,1536]{2,1,0:T(8,128)(2,1)} %stack.2), calls=%async_computation | async-start | bytes 12582912 | tf_op jit(solution)/shard_map/all_to_all | solution.py:78
  27.0 3.5 collective-permute-start
  30.5 2.0 collective-permute-start.1
  33.7 150.8 %collective-permute-done = bf16[128,1536]{1,0:T(8,128)(2,1)S(1)} collective-permute-done((bf16[128,1536]{1,0:T(8,128)(2,1)S(1)}, bf16[128,1536]{1,0:T(8,128)(2,1)S(1)}, u32[]{:S(2)}, u32[]{:S(2)}) %collective-permute-start) | collective-permute-done | bytes 393248 | tf_op jit(solution)/shard_map/ppermute | solution.py:15
  184.5 4.4 %collective-permute-start.2 = (bf16[128,1536]{1,0:T(8,128)(2,1)S(1)}, bf16[128,1536]{1,0:T(8,128)(2,1)}, u32[]{:S(2)}, u32[]{:S(2)}) collective-permute-start(bf16[128,1536]{1,0:T(8,128)(2,1)S(1)} %collective-permute-done), channel_id=1, source_target_pairs={{0,2},{2,4},{4,6},{6,8},{8,10},{10,12},{12,14},{14,16},{16,18},{18... | collective-permute-start | bytes 1179656 | tf_op jit(solution)/shard_map/ppermute | solution.py:15
  189.4 4.4 %collective-permute-start.3 = (bf16[128,1536]{1,0:T(8,128)(2,1)S(1)}, bf16[128,1536]{1,0:T(8,128)(2,1)}, u32[]{:S(2)}, u32[]{:S(2)}) collective-permute-start(bf16[128,1536]{1,0:T(8,128)(2,1)S(1)} %collective-permute-done.1), channel_id=1, source_target_pairs={{0,2},{2,4},{4,6},{6,8},{8,10},{10,12},{12,14},{14,16},{16,18},{18... | collective-permute-start | bytes 1179656 | tf_op jit(solution)/shard_map/ppermute | solution.py:15
  194.4 3.8 collective-permute-start.4
  199.1 4.6 %collective-permute-start.5 = (bf16[128,1536]{1,0:T(8,128)(2,1)}, bf16[128,1536]{1,0:T(8,128)(2,1)}, u32[]{:S(2)}, u32[]{:S(2)}) collective-permute-start(bf16[128,1536]{1,0:T(8,128)(2,1)} %collective-permute-done.3), channel_id=1, source_target_pairs={{0,2},{2,4},{4,6},{6,8},{8,10},{10,12},{12,14},{14,16},{16,18},{18... | collective-permute-start | bytes 1179656 | tf_op jit(solution)/shard_map/ppermute | solution.py:15
  206.6 1.9 collective-permute-start.6
  209.3 4.4 %collective-permute-start.7 = (bf16[128,1536]{1,0:T(8,128)(2,1)}, bf16[128,1536]{1,0:T(8,128)(2,1)S(1)}, u32[]{:S(2)}, u32[]{:S(2)}) collective-permute-start(bf16[128,1536]{1,0:T(8,128)(2,1)} %collective-permute-done.5), channel_id=1, source_target_pairs={{0,2},{2,4},{4,6},{6,8},{8,10},{10,12},{12,14},{14,16},{16,18},{18... | collective-permute-start | bytes 1179656 | tf_op jit(solution)/shard_map/ppermute | solution.py:15
  214.7 3.9 %collective-permute-start.8 = (bf16[128,1536]{1,0:T(8,128)(2,1)}, bf16[128,1536]{1,0:T(8,128)(2,1)}, u32[]{:S(2)}, u32[]{:S(2)}) collective-permute-start(bf16[128,1536]{1,0:T(8,128)(2,1)} %collective-permute-done.6), channel_id=1, source_target_pairs={{0,2},{2,4},{4,6},{6,8},{8,10},{10,12},{12,14},{14,16},{16,18},{18... | collective-permute-start | bytes 1179656 | tf_op jit(solution)/shard_map/ppermute | solution.py:15
  218.7 4.3 %collective-permute-start.9 = (bf16[128,1536]{1,0:T(8,128)(2,1)S(1)}, bf16[128,1536]{1,0:T(8,128)(2,1)}, u32[]{:S(2)}, u32[]{:S(2)}) collective-permute-start(bf16[128,1536]{1,0:T(8,128)(2,1)S(1)} %collective-permute-done.7), channel_id=1, source_target_pairs={{0,2},{2,4},{4,6},{6,8},{8,10},{10,12},{12,14},{14,16},{16,18},{18... | collective-permute-start | bytes 1179656 | tf_op jit(solution)/shard_map/ppermute | solution.py:15
  225.4 1.2 copy.101
  226.6 2.1 collective-permute-start.10
  228.7 4.3 %collective-permute-start.11 = (bf16[128,1536]{1,0:T(8,128)(2,1)}, bf16[128,1536]{1,0:T(8,128)(2,1)}, u32[]{:S(2)}, u32[]{:S(2)}) collective-permute-start(bf16[128,1536]{1,0:T(8,128)(2,1)} %collective-permute-done.9), channel_id=1, source_target_pairs={{0,2},{2,4},{4,6},{6,8},{8,10},{10,12},{12,14},{14,16},{16,18},{18... | collective-permute-start | bytes 1179656 | tf_op jit(solution)/shard_map/ppermute | solution.py:15
  233.1 2.0 fusion.170
  235.1 1.9 copy.102
  237.0 1.2 copy.104
  238.2 1.9 copy.105
  240.1 1.9 fusion.169
  242.1 1.2 copy.107
  243.3 2.3 collective-permute-start.12
  245.6 4.3 %collective-permute-start.13 = (bf16[128,1536]{1,0:T(8,128)(2,1)}, bf16[128,1536]{1,0:T(8,128)(2,1)}, u32[]{:S(2)}, u32[]{:S(2)}) collective-permute-start(bf16[128,1536]{1,0:T(8,128)(2,1)} %collective-permute-done.11), channel_id=1, source_target_pairs={{0,2},{2,4},{4,6},{6,8},{8,10},{10,12},{12,14},{14,16},{16,18},{18... | collective-permute-start | bytes 1179656 | tf_op jit(solution)/shard_map/ppermute | solution.py:15
  249.9 1.9 fusion.168
  252.8 1.2 copy.110
  254.0 1.9 copy.111
  255.9 2.0 fusion.167
  257.9 1.2 copy.113
  259.1 4.7 %collective-permute-start.14 = (bf16[128,1536]{1,0:T(8,128)(2,1)}, bf16[128,1536]{1,0:T(8,128)(2,1)S(1)}, u32[]{:S(2)}, u32[]{:S(2)}) collective-permute-start(bf16[128,1536]{1,0:T(8,128)(2,1)} %collective-permute-done.12), channel_id=1, source_target_pairs={{0,2},{2,4},{4,6},{6,8},{8,10},{10,12},{12,14},{14,16},{16,18},{18... | collective-permute-start | bytes 1179656 | tf_op jit(solution)/shard_map/ppermute | solution.py:15
  263.8 4.6 %collective-permute-start.15 = (bf16[128,1536]{1,0:T(8,128)(2,1)}, bf16[128,1536]{1,0:T(8,128)(2,1)}, u32[]{:S(2)}, u32[]{:S(2)}) collective-permute-start(bf16[128,1536]{1,0:T(8,128)(2,1)} %collective-permute-done.13), channel_id=1, source_target_pairs={{0,2},{2,4},{4,6},{6,8},{8,10},{10,12},{12,14},{14,16},{16,18},{18... | collective-permute-start | bytes 1179656 | tf_op jit(solution)/shard_map/ppermute | solution.py:15
  268.4 1.9 fusion.166
  270.3 1.9 copy.114
  272.3 1.2 copy.116
  273.5 1.9 copy.117
  275.4 2.0 fusion.165
  277.6 1.9 copy.120
  279.5 1.9 fusion.164
  281.5 13.6 %reshape_reshape.3 = bf16[2048,16,96]{2,1,0:T(8,128)(2,1)} reshape(bf16[128,16,1536]{2,1,0:T(8,128)(2,1)} %all-to-all-done) | data formatting | bytes 12582912 | tf_op jit(solution)/shard_map/reshape;reshape | solution.py:44
  295.1 10.1 %fusion = (f32[16,128]{1,0:T(8,128)}, f32[16,128,2048]{2,1,0:T(8,128)S(1)}) fusion(pred[128,2048]{1,0:T(8,128)(4,1)} %compare_and_fusion, bf16[128,16,96]{0,2,1:T(8,128)(2,1)S(1)} %bitcast.299, bf16[2048,16,96]{2,1,0:T(8,128)(2,1)} %reshape_reshape.3), kind=kOutput, calls=%fused_computation.2 | convolution fusion | flops 817887232 | bytes 23732224 | tf_op jit(solution)/shard_map/shd,khd->hsk/dot_general | solution.py:47
  305.2 2.2 bitcast_maximum_fusion.3
  307.4 2.5 fusion.162
  311.2 6.6 %fusion.1 = f32[16,128]{1,0:T(8,128)} fusion(f32[16,128,2048]{2,1,0:T(8,128)S(1)} %get-tuple-element.97, f32[16,128]{1,0:T(8,128)S(1)} %get-tuple-element.62, pred[128,2048]{1,0:T(8,128)(4,1)} %compare_and_fusion), kind=kLoop, calls=%fused_computation.3 | loop fusion | flops 20969472 | bytes 17055744 | tf_op jit(solution)/shard_map/reduce_sum | solution.py:53
  317.8 8.7 %copy.94 = bf16[2048,1536]{0,1:T(8,128)(2,1)} copy(bf16[2048,1536]{1,0:T(8,128)(2,1)} %all-gather.2.cloned.1.call-done) | data formatting | bytes 12582912 | tf_op jit(solution)/shard_map/all_gather | solution.py:80
  326.8 10.3 %fusion.40 = f32[128,16,96]{0,2,1:T(8,128)S(1)} fusion(bf16[2048,16,96]{0,2,1:T(8,128)(2,1)} %bitcast.302, f32[16,128,2048]{2,1,0:T(8,128)} %copy-done, f32[16,128]{1,0:T(8,128)} %copy-done.46, pred[128,2048]{1,0:T(8,128)(4,1)S(1)} %copy-done.7), kind=kOutput, calls=%fused_computation.61 | convolution fusion | flops 826277888 | bytes 24125440 | tf_op jit(solution)/shard_map/hsk,khd->hsd/dot_general | solution.py:54
  345.4 2.3 fusion.8
  347.7 22.3 %reduce-scatter.2.cloned.1.call-done = bf16[1536,128]{0,1:T(8,128)(2,1)} async-done(((bf16[3072,128]{0,1:T(8,128)(2,1)}), bf16[1536,128]{0,1:T(8,128)(2,1)}) %reduce-scatter.2.cloned.1.call-update) | async-done | bytes 393232 | tf_op jit(solution)/shard_map/reduce_scatter | solution.py:98
  370.0 1.9 copy.122
  (198 shorter events, 21.2 us)
Async XLA Ops:
  6.5 20.4 %copy-start.18 = (bf16[128,1536]{1,0:T(8,128)(2,1)S(1)}, bf16[128,1536]{1,0:T(8,128)(2,1)}, u32[]{:S(2)}) copy-start(bf16[128,1536]{1,0:T(8,128)(2,1)} %param.11) | copy-start | bytes 1179652
  6.5 24.0 %copy-start.19 = (bf16[128,1536]{1,0:T(8,128)(2,1)S(1)}, bf16[128,1536]{1,0:T(8,128)(2,1)}, u32[]{:S(2)}) copy-start(bf16[128,1536]{1,0:T(8,128)(2,1)} %param.12) | copy-start | bytes 1179652
  6.5 26.0 %copy-start.51 = (s32[32]{0:T(128)S(1)}, s32[32]{0:T(128)}, u32[]{:S(2)}) copy-start(s32[32]{0:T(128)} %param.17) | copy-start | bytes 388
  6.5 26.4 %copy-start.52 = (s32[32]{0:T(128)S(1)}, s32[32]{0:T(128)}, u32[]{:S(2)}) copy-start(s32[32]{0:T(128)} %param.18) | copy-start | bytes 388
  6.5 187.3 %copy-start.17 = (bf16[128,1536]{1,0:T(8,128)(2,1)S(1)}, bf16[128,1536]{1,0:T(8,128)(2,1)}, u32[]{:S(2)}) copy-start(bf16[128,1536]{1,0:T(8,128)(2,1)} %param.10) | copy-start | bytes 1179652
  6.5 187.5 %copy-start.48 = (bf16[8,1536]{1,0:T(8,128)(2,1)S(1)}, bf16[8,1536]{1,0:T(8,128)(2,1)}, u32[]{:S(2)}) copy-start(bf16[8,1536]{1,0:T(8,128)(2,1)} %param.15) | copy-start | bytes 73732
  6.6 198.3 %copy-start.49 = (bf16[8,1536]{1,0:T(8,128)(2,1)S(1)}, bf16[8,1536]{1,0:T(8,128)(2,1)}, u32[]{:S(2)}) copy-start(bf16[8,1536]{1,0:T(8,128)(2,1)} %param.16) | copy-start | bytes 73732
  10.9 270.5 %all-to-all-start = ((bf16[128,16,1536]{2,1,0:T(8,128)(2,1)}), bf16[128,16,1536]{2,1,0:T(8,128)(2,1)}, u32[]{:S(2)}, u32[]{:S(2)}) async-start(bf16[128,16,1536]{2,1,0:T(8,128)(2,1)} %stack.2), calls=%async_computation | async-start | bytes 12582912 | tf_op jit(solution)/shard_map/all_to_all | solution.py:78
  26.2 291.6 %all-gather.2.cloned.1.call-start = ((), (), s32[]{:S(2)}) async-start(), calls=%async_computation.2 | async-start | bytes 6340608 | tf_op jit(solution)/shard_map/all_gather | solution.py:80
  26.9 343.1 %reduce-scatter.2.cloned.1.call-start = ((), (), s32[]{:S(2)}) async-start(), calls=%async_computation.3 | async-start | bytes 1179648 | tf_op jit(solution)/shard_map/reduce_scatter | solution.py:98
  27.0 157.5 %collective-permute-start = (bf16[128,1536]{1,0:T(8,128)(2,1)S(1)}, bf16[128,1536]{1,0:T(8,128)(2,1)S(1)}, u32[]{:S(2)}, u32[]{:S(2)}) collective-permute-start(bf16[128,1536]{1,0:T(8,128)(2,1)S(1)} %copy-done.18), channel_id=1, source_target_pairs={{0,2},{2,4},{4,6},{6,8},{8,10},{10,12},{12,14},{14,16},{16,18},{18... | collective-permute-start | bytes 1179656 | tf_op jit(solution)/shard_map/ppermute | solution.py:15
  30.5 158.9 %collective-permute-start.1 = (bf16[128,1536]{1,0:T(8,128)(2,1)S(1)}, bf16[128,1536]{1,0:T(8,128)(2,1)S(1)}, u32[]{:S(2)}, u32[]{:S(2)}) collective-permute-start(bf16[128,1536]{1,0:T(8,128)(2,1)S(1)} %copy-done.19), channel_id=1, source_target_pairs={{0,2},{2,4},{4,6},{6,8},{8,10},{10,12},{12,14},{14,16},{16,18},{18... | collective-permute-start | bytes 1179656 | tf_op jit(solution)/shard_map/ppermute | solution.py:15
  33.2 248.2 %copy-start.50 = (pred[128,8]{0,1:T(8,128)(4,1)}, pred[128,8]{0,1:T(8,128)(4,1)S(1)}, u32[]{:S(2)}) copy-start(pred[128,8]{0,1:T(8,128)(4,1)S(1)} %broadcast_compare_fusion) | copy-start | bytes 3076
  33.7 189.3 %copy-start.25 = (pred[128,128]{0,1:T(8,128)(4,1)}, pred[128,128]{0,1:T(8,128)(4,1)S(1)}, u32[]{:S(2)}) copy-start(pred[128,128]{0,1:T(8,128)(4,1)S(1)} %get-tuple-element.69) | copy-start | bytes 49156
  33.7 247.8 %copy-start.21 = (pred[128,128]{0,1:T(8,128)(4,1)}, pred[128,128]{0,1:T(8,128)(4,1)S(1)}, u32[]{:S(2)}) copy-start(pred[128,128]{0,1:T(8,128)(4,1)S(1)} %get-tuple-element.73) | copy-start | bytes 49156
  33.7 247.8 %copy-start.23 = (pred[128,128]{0,1:T(8,128)(4,1)}, pred[128,128]{0,1:T(8,128)(4,1)S(1)}, u32[]{:S(2)}) copy-start(pred[128,128]{0,1:T(8,128)(4,1)S(1)} %get-tuple-element.71) | copy-start | bytes 49156
  184.5 9.9 %collective-permute-start.2 = (bf16[128,1536]{1,0:T(8,128)(2,1)S(1)}, bf16[128,1536]{1,0:T(8,128)(2,1)}, u32[]{:S(2)}, u32[]{:S(2)}) collective-permute-start(bf16[128,1536]{1,0:T(8,128)(2,1)S(1)} %collective-permute-done), channel_id=1, source_target_pairs={{0,2},{2,4},{4,6},{6,8},{8,10},{10,12},{12,14},{14,16},{16,18},{18... | collective-permute-start | bytes 1179656 | tf_op jit(solution)/shard_map/ppermute | solution.py:15
  189.4 9.7 %collective-permute-start.3 = (bf16[128,1536]{1,0:T(8,128)(2,1)S(1)}, bf16[128,1536]{1,0:T(8,128)(2,1)}, u32[]{:S(2)}, u32[]{:S(2)}) collective-permute-start(bf16[128,1536]{1,0:T(8,128)(2,1)S(1)} %collective-permute-done.1), channel_id=1, source_target_pairs={{0,2},{2,4},{4,6},{6,8},{8,10},{10,12},{12,14},{14,16},{16,18},{18... | collective-permute-start | bytes 1179656 | tf_op jit(solution)/shard_map/ppermute | solution.py:15
  194.4 12.2 %collective-permute-start.4 = (bf16[128,1536]{1,0:T(8,128)(2,1)}, bf16[128,1536]{1,0:T(8,128)(2,1)}, u32[]{:S(2)}, u32[]{:S(2)}) collective-permute-start(bf16[128,1536]{1,0:T(8,128)(2,1)} %collective-permute-done.2), channel_id=1, source_target_pairs={{0,2},{2,4},{4,6},{6,8},{8,10},{10,12},{12,14},{14,16},{16,18},{18... | collective-permute-start | bytes 1179656 | tf_op jit(solution)/shard_map/ppermute | solution.py:15
  199.1 10.1 %collective-permute-start.5 = (bf16[128,1536]{1,0:T(8,128)(2,1)}, bf16[128,1536]{1,0:T(8,128)(2,1)}, u32[]{:S(2)}, u32[]{:S(2)}) collective-permute-start(bf16[128,1536]{1,0:T(8,128)(2,1)} %collective-permute-done.3), channel_id=1, source_target_pairs={{0,2},{2,4},{4,6},{6,8},{8,10},{10,12},{12,14},{14,16},{16,18},{18... | collective-permute-start | bytes 1179656 | tf_op jit(solution)/shard_map/ppermute | solution.py:15
  206.6 8.1 %collective-permute-start.6 = (bf16[128,1536]{1,0:T(8,128)(2,1)}, bf16[128,1536]{1,0:T(8,128)(2,1)}, u32[]{:S(2)}, u32[]{:S(2)}) collective-permute-start(bf16[128,1536]{1,0:T(8,128)(2,1)} %collective-permute-done.4), channel_id=1, source_target_pairs={{0,2},{2,4},{4,6},{6,8},{8,10},{10,12},{12,14},{14,16},{16,18},{18... | collective-permute-start | bytes 1179656 | tf_op jit(solution)/shard_map/ppermute | solution.py:15
  209.3 9.4 %collective-permute-start.7 = (bf16[128,1536]{1,0:T(8,128)(2,1)}, bf16[128,1536]{1,0:T(8,128)(2,1)S(1)}, u32[]{:S(2)}, u32[]{:S(2)}) collective-permute-start(bf16[128,1536]{1,0:T(8,128)(2,1)} %collective-permute-done.5), channel_id=1, source_target_pairs={{0,2},{2,4},{4,6},{6,8},{8,10},{10,12},{12,14},{14,16},{16,18},{18... | collective-permute-start | bytes 1179656 | tf_op jit(solution)/shard_map/ppermute | solution.py:15
  214.7 11.9 %collective-permute-start.8 = (bf16[128,1536]{1,0:T(8,128)(2,1)}, bf16[128,1536]{1,0:T(8,128)(2,1)}, u32[]{:S(2)}, u32[]{:S(2)}) collective-permute-start(bf16[128,1536]{1,0:T(8,128)(2,1)} %collective-permute-done.6), channel_id=1, source_target_pairs={{0,2},{2,4},{4,6},{6,8},{8,10},{10,12},{12,14},{14,16},{16,18},{18... | collective-permute-start | bytes 1179656 | tf_op jit(solution)/shard_map/ppermute | solution.py:15
  218.7 10.0 %collective-permute-start.9 = (bf16[128,1536]{1,0:T(8,128)(2,1)S(1)}, bf16[128,1536]{1,0:T(8,128)(2,1)}, u32[]{:S(2)}, u32[]{:S(2)}) collective-permute-start(bf16[128,1536]{1,0:T(8,128)(2,1)S(1)} %collective-permute-done.7), channel_id=1, source_target_pairs={{0,2},{2,4},{4,6},{6,8},{8,10},{10,12},{12,14},{14,16},{16,18},{18... | collective-permute-start | bytes 1179656 | tf_op jit(solution)/shard_map/ppermute | solution.py:15
  223.2 58.3 %copy-start.27 = (pred[128,128]{0,1:T(8,128)(4,1)}, pred[128,128]{0,1:T(8,128)(4,1)S(1)}, u32[]{:S(2)}) copy-start(pred[128,128]{0,1:T(8,128)(4,1)S(1)} %get-tuple-element.76) | copy-start | bytes 49156
  226.6 16.7 %collective-permute-start.10 = (bf16[128,1536]{1,0:T(8,128)(2,1)}, bf16[128,1536]{1,0:T(8,128)(2,1)}, u32[]{:S(2)}, u32[]{:S(2)}) collective-permute-start(bf16[128,1536]{1,0:T(8,128)(2,1)} %collective-permute-done.8), channel_id=1, source_target_pairs={{0,2},{2,4},{4,6},{6,8},{8,10},{10,12},{12,14},{14,16},{16,18},{18... | collective-permute-start | bytes 1179656 | tf_op jit(solution)/shard_map/ppermute | solution.py:15
  228.7 16.9 %collective-permute-start.11 = (bf16[128,1536]{1,0:T(8,128)(2,1)}, bf16[128,1536]{1,0:T(8,128)(2,1)}, u32[]{:S(2)}, u32[]{:S(2)}) collective-permute-start(bf16[128,1536]{1,0:T(8,128)(2,1)} %collective-permute-done.9), channel_id=1, source_target_pairs={{0,2},{2,4},{4,6},{6,8},{8,10},{10,12},{12,14},{14,16},{16,18},{18... | collective-permute-start | bytes 1179656 | tf_op jit(solution)/shard_map/ppermute | solution.py:15
  243.3 15.8 %collective-permute-start.12 = (bf16[128,1536]{1,0:T(8,128)(2,1)}, bf16[128,1536]{1,0:T(8,128)(2,1)}, u32[]{:S(2)}, u32[]{:S(2)}) collective-permute-start(bf16[128,1536]{1,0:T(8,128)(2,1)} %collective-permute-done.10), channel_id=1, source_target_pairs={{0,2},{2,4},{4,6},{6,8},{8,10},{10,12},{12,14},{14,16},{16,18},{18... | collective-permute-start | bytes 1179656 | tf_op jit(solution)/shard_map/ppermute | solution.py:15
  245.6 18.2 %collective-permute-start.13 = (bf16[128,1536]{1,0:T(8,128)(2,1)}, bf16[128,1536]{1,0:T(8,128)(2,1)}, u32[]{:S(2)}, u32[]{:S(2)}) collective-permute-start(bf16[128,1536]{1,0:T(8,128)(2,1)} %collective-permute-done.11), channel_id=1, source_target_pairs={{0,2},{2,4},{4,6},{6,8},{8,10},{10,12},{12,14},{14,16},{16,18},{18... | collective-permute-start | bytes 1179656 | tf_op jit(solution)/shard_map/ppermute | solution.py:15
  259.1 18.3 %collective-permute-start.14 = (bf16[128,1536]{1,0:T(8,128)(2,1)}, bf16[128,1536]{1,0:T(8,128)(2,1)S(1)}, u32[]{:S(2)}, u32[]{:S(2)}) collective-permute-start(bf16[128,1536]{1,0:T(8,128)(2,1)} %collective-permute-done.12), channel_id=1, source_target_pairs={{0,2},{2,4},{4,6},{6,8},{8,10},{10,12},{12,14},{14,16},{16,18},{18... | collective-permute-start | bytes 1179656 | tf_op jit(solution)/shard_map/ppermute | solution.py:15
  263.8 13.8 %collective-permute-start.15 = (bf16[128,1536]{1,0:T(8,128)(2,1)}, bf16[128,1536]{1,0:T(8,128)(2,1)}, u32[]{:S(2)}, u32[]{:S(2)}) collective-permute-start(bf16[128,1536]{1,0:T(8,128)(2,1)} %collective-permute-done.13), channel_id=1, source_target_pairs={{0,2},{2,4},{4,6},{6,8},{8,10},{10,12},{12,14},{14,16},{16,18},{18... | collective-permute-start | bytes 1179656 | tf_op jit(solution)/shard_map/ppermute | solution.py:15
  305.2 21.2 %copy-start.7 = (pred[128,2048]{1,0:T(8,128)(4,1)S(1)}, pred[128,2048]{1,0:T(8,128)(4,1)}, u32[]{:S(2)}) copy-start(pred[128,2048]{1,0:T(8,128)(4,1)} %compare_and_fusion) | copy-start | bytes 786436
  310.0 16.5 %copy-start.46 = (f32[16,128]{1,0:T(8,128)}, f32[16,128]{1,0:T(8,128)S(1)}, u32[]{:S(2)}) copy-start(f32[16,128]{1,0:T(8,128)S(1)} %get-tuple-element.62) | copy-start | bytes 24580
  326.6 12.1 %copy-start.38 = (f32[16,128]{1,0:T(8,128)S(1)}, f32[16,128]{1,0:T(8,128)}, u32[]{:S(2)}) copy-start(f32[16,128]{1,0:T(8,128)} %get-tuple-element.60) | copy-start | bytes 24580
  326.6 12.3 %copy-start.26 = (pred[128,128]{0,1:T(8,128)(4,1)S(1)}, pred[128,128]{0,1:T(8,128)(4,1)}, u32[]{:S(2)}) copy-start(pred[128,128]{0,1:T(8,128)(4,1)} %copy-done.25) | copy-start | bytes 49156
  326.6 12.3 %copy-start.39 = (f32[16,128]{1,0:T(8,128)S(1)}, f32[16,128]{1,0:T(8,128)}, u32[]{:S(2)}) copy-start(f32[16,128]{1,0:T(8,128)} %get-tuple-element.61) | copy-start | bytes 24580
  326.6 12.5 %copy-start.44 = (f32[16,128]{1,0:T(8,128)S(1)}, f32[16,128]{1,0:T(8,128)}, u32[]{:S(2)}) copy-start(f32[16,128]{1,0:T(8,128)} %get-tuple-element.68) | copy-start | bytes 24580
  326.6 13.4 %copy-start.29 = (f32[16,128]{1,0:T(8,128)S(1)}, f32[16,128]{1,0:T(8,128)}, u32[]{:S(2)}) copy-start(f32[16,128]{1,0:T(8,128)} %get-tuple-element.92) | copy-start | bytes 24580
  326.6 13.4 %copy-start.30 = (f32[16,128]{1,0:T(8,128)S(1)}, f32[16,128]{1,0:T(8,128)}, u32[]{:S(2)}) copy-start(f32[16,128]{1,0:T(8,128)} %get-tuple-element.88) | copy-start | bytes 24580
  326.7 13.4 %copy-start.32 = (f32[16,128]{1,0:T(8,128)S(1)}, f32[16,128]{1,0:T(8,128)}, u32[]{:S(2)}) copy-start(f32[16,128]{1,0:T(8,128)} %get-tuple-element.96) | copy-start | bytes 24580
  326.7 13.4 %copy-start.40 = (f32[16,128]{1,0:T(8,128)S(1)}, f32[16,128]{1,0:T(8,128)}, u32[]{:S(2)}) copy-start(f32[16,128]{1,0:T(8,128)} %get-tuple-element.84) | copy-start | bytes 24580
  326.7 13.4 %copy-start.41 = (f32[16,128]{1,0:T(8,128)S(1)}, f32[16,128]{1,0:T(8,128)}, u32[]{:S(2)}) copy-start(f32[16,128]{1,0:T(8,128)} %get-tuple-element.82) | copy-start | bytes 24580
  326.7 13.4 %copy-start.42 = (f32[16,128]{1,0:T(8,128)S(1)}, f32[16,128]{1,0:T(8,128)}, u32[]{:S(2)}) copy-start(f32[16,128]{1,0:T(8,128)} %get-tuple-element.80) | copy-start | bytes 24580
  326.7 13.4 %copy-start.43 = (f32[16,128]{1,0:T(8,128)S(1)}, f32[16,128]{1,0:T(8,128)}, u32[]{:S(2)}) copy-start(f32[16,128]{1,0:T(8,128)} %get-tuple-element.78) | copy-start | bytes 24580
  326.7 13.4 %copy-start.45 = (f32[16,128]{1,0:T(8,128)S(1)}, f32[16,128]{1,0:T(8,128)}, u32[]{:S(2)}) copy-start(f32[16,128]{1,0:T(8,128)} %fusion.1) | copy-start | bytes 24580
  326.7 14.2 %copy-start.31 = (bf16[8,16,96]{2,1,0:T(8,128)(2,1)S(1)}, bf16[8,16,96]{2,1,0:T(8,128)(2,1)}, u32[]{:S(2)}) copy-start(bf16[8,16,96]{2,1,0:T(8,128)(2,1)} %reshape.1639) | copy-start | bytes 73732
  326.7 15.3 %copy-start.9 = (bf16[128,1536]{0,1:T(8,128)(2,1)S(1)}, bf16[128,1536]{0,1:T(8,128)(2,1)}, u32[]{:S(2)}) copy-start(bf16[128,1536]{0,1:T(8,128)(2,1)} %copy.96) | copy-start | bytes 1179652
  326.7 15.6 %copy-start.10 = (bf16[128,1536]{0,1:T(8,128)(2,1)S(1)}, bf16[128,1536]{0,1:T(8,128)(2,1)}, u32[]{:S(2)}) copy-start(bf16[128,1536]{0,1:T(8,128)(2,1)} %copy.99) | copy-start | bytes 1179652
  (27 other events, 242.8 us)
Sparse Core Ops, SparseCore 0:
  28.8 288.1 all-gather.1
  347.8 22.1 reduce-scatter.1
